TPU v7x, 256 devices: a whole 4x4x8 slice. The times are simulated.
256 devices in a mesh: rep: 128 (over z, y, x_hi, core), shard: 2 (over x_lo).
Axes of the slice: x: 4 (x_hi: 2, x_lo: 2; x = x_hi * 2 + x_lo), y: 4, z: 8, core: 2. Of those that a mesh axis runs over, the one named last changes fastest.
Arguments:
- grads: float32 [128, 4, 384, 1536], P('rep', None, 'shard'), may hold values from -6 to 6
- basis: float32 [4, 384, 128], P(None, 'shard'), may hold values from -0.3125 to 0.3125
- weights: float32 [4, 384, 1536], P(None, 'shard'), may hold values from -0.3125 to 0.3125
- first_moment: float32 [4, 128, 1536], P(None, 'shard'), may hold values from -6 to 6
- second_moment: float32 [4, 128, 1536], P(None, 'shard'), may hold values from 0.01 to 1
Outputs:
- new_weights: float32 [4, 384, 1536], P(None, 'shard')
- new_first: float32 [4, 128, 1536], P(None, 'shard')
- new_second: float32 [4, 128, 1536], P(None, 'shard')
- new_basis: float32 [4, 384, 128], P(None, 'shard')
All inputs are finite; a program needn't handle non-finite values.
Results may differ from a plain program's by a relative error of at most 0.000057.
Values sent between devices are 32-bit elements; how exact they have to be, the bound alone decides.
No kernel may reach another device: no remote copies, remote signals or barrier semaphores. Data moves between devices by JAX's collectives and lax.ppermute only.
A program may use at most 128 MiB of HBM per device.

v0:
```python
import jax
import jax.numpy as jnp
from jax import lax
from jax.sharding import Mesh, PartitionSpec as P

ADAM_STEP = 100
HIGH = lax.Precision.HIGHEST
SIZES = {"z": 8, "y": 4, "xh": 2, "core": 2, "xl": 2}
REP = ("z", "y", "xh", "core")


def shift(x, axis, k):
    n = SIZES[axis]
    return lax.ppermute(x, axis, [(i, (i + k) % n) for i in range(n)])


def flip(x, axis, bit=1):
    n = SIZES[axis]
    return lax.ppermute(x, axis, [(i, i ^ bit) for i in range(n)])


def rows(x, index, count):
    return lax.dynamic_slice_in_dim(x, index * count, count, 0)


def in_order(index, mine, other):
    first = index == 0
    return (jnp.where(first, mine, other), jnp.where(first, other, mine))


def scatter_direct(x, axis):
    n, me = (SIZES[axis], lax.axis_index(axis))
    count = x.shape[0] // n
    total = rows(x, me, count)
    for k in range(1, n):
        total = total + shift(rows(x, (me + k) % n, count), axis, k)
    return total


def gather_direct(x, axis):
    n, me = (SIZES[axis], lax.axis_index(axis))
    count = x.shape[0]
    out = jnp.zeros((n * count,) + x.shape[1:], x.dtype)
    out = lax.dynamic_update_slice_in_dim(out, x, me * count, 0)
    for k in range(1, n):
        out = lax.dynamic_update_slice_in_dim(out, shift(x, axis, k), (me - k) % n * count, 0)
    return out


def scatter_exchange(x, axis):
    n = SIZES[axis]
    parts = x.reshape((n, x.shape[0] // n) + x.shape[1:])
    return jnp.sum(lax.all_to_all(parts, axis, split_axis=0, concat_axis=0), axis=0)


def on_device(grads, basis, weights, first_moment, second_moment):
    layers, depth, width = grads.shape[1:]
    rank = basis.shape[2]
    half = layers // 2
    piece = width // 64
    z, y, xh = (lax.axis_index("z"), lax.axis_index("y"), lax.axis_index("xh"))
    core, xl = (lax.axis_index("core"), lax.axis_index("xl"))
    place = (y * 2 + xh) * 8 + z
    given = flip(rows(grads[0], 1 - core, half), "core")
    pair = rows(grads[0], core, half) + given
    held = pair.reshape(half * depth, width).T
    held = scatter_direct(held, "y")
    held = scatter_direct(held, "xh")
    total = scatter_exchange(held, "z").reshape(piece, half, depth)
    basis_pair = rows(basis, core, half)
    cut = [
        jnp.swapaxes(
            lax.dynamic_slice(m, (core * half, 0, place * piece), (half, rank // 2, piece)), 1, 2
        )
        for m in (first_moment, second_moment)
    ]
    cut = jnp.concatenate(cut, axis=2)
    low, high = in_order(xl, cut, flip(cut, "xl"))
    first = jnp.concatenate([low[:, :, : rank // 2], high[:, :, : rank // 2]], axis=2)
    second = jnp.concatenate([low[:, :, rank // 2 :], high[:, :, rank // 2 :]], axis=2)
    proj = jnp.einsum("fld,ldr->lfr", total, basis_pair, precision=HIGH)
    proj = proj + flip(proj, "xl")
    new_first = 0.9 * first + 0.1 * proj
    new_second = 0.999 * second + 0.001 * proj * proj
    direction = (
        new_first
        / (1.0 - 0.9**ADAM_STEP)
        / (jnp.sqrt(new_second / (1.0 - 0.999**ADAM_STEP)) + 1e-08)
    )
    mine = jnp.where(xl == 0, proj[:, :, : rank // 2], proj[:, :, rank // 2 :])
    packed = jnp.concatenate([direction[0], direction[1], mine[0], mine[1]], axis=1)
    refresh = jnp.einsum("fld,lfr->ldr", total, proj, precision=HIGH)
    part = scatter_exchange(refresh.reshape(half * depth, rank), "z")
    part = part + flip(part, "y", 1)
    part = part + flip(part, "y", 2)
    part = part + flip(part, "xh")
    refresh = lax.all_gather(part, "z", axis=0, tiled=True).reshape(half, depth, rank)
    gram = jnp.einsum("ldr,lds->lrs", refresh, refresh, precision=HIGH)
    gram = gram + flip(gram, "xl")
    sumsq = jnp.einsum("lrr->l", gram)
    factor = jnp.sqrt(jnp.float32(rank)) / (2.0 * jnp.sqrt(sumsq + 1e-06))
    scaled = refresh * factor[:, None, None]
    gram_scaled = gram * (factor * factor)[:, None, None]
    basis_new = 1.5 * scaled - 0.5 * jnp.einsum("ldr,lrs->lds", scaled, gram_scaled, precision=HIGH)
    new_basis = jnp.concatenate(in_order(core, basis_new, flip(basis_new, "core")), axis=0)
    packed = lax.all_gather(packed, "z", axis=0, tiled=True)
    packed = gather_direct(packed, "xh")
    packed = gather_direct(packed, "y")
    packed = jnp.stack(in_order(core, packed, flip(packed, "core")))
    dirs = packed[:, :, : half * rank].reshape(2, width, half, rank)
    own = packed[:, :, half * rank :].reshape(2, width, half, rank // 2)
    own = jnp.transpose(own, (0, 2, 3, 1)).reshape(layers, rank // 2, width)
    new_first = 0.9 * first_moment + 0.1 * own
    new_second = 0.999 * second_moment + 0.001 * own * own
    dirs = jnp.transpose(dirs, (0, 2, 1, 3)).reshape(layers, width, rank)
    update = jnp.einsum("ldr,lfr->ldf", basis, dirs, precision=HIGH)
    new_weights = weights - 0.0125 * update
    return (new_weights, new_first, new_second, new_basis)


def solution(mesh):
    fine = Mesh(mesh.devices.reshape(8, 4, 2, 2, 2), ("z", "y", "xh", "core", "xl"))
    split = P(None, "xl", None)
    return jax.shard_map(
        on_device,
        mesh=fine,
        in_specs=(P(REP, None, "xl", None), split, split, split, split),
        out_specs=(split, split, split, split),
        check_vma=False,
    )
```

profile of v0, /device:TPU:1, one launch (start us, length us, event | category | flops | bytes accessed | tf_op | source)
XLA Modules:
  0.0 224.6 jit_solution(4249226077808333504)
XLA Ops:
  0.7 1.9 dynamic-slice_bitcast_fusion
  2.5 3.3 %collective-permute-start.1 = (f32[2,192,1536]{2,1,0:T(8,128)S(1)}, f32[2,192,1536]{2,1,0:T(8,128)}, u32[]{:S(2)}, u32[]{:S(2)}) collective-permute-start(f32[2,192,1536]{2,1,0:T(8,128)S(1)} %dynamic-slice_bitcast_fusion), channel_id=1, source_target_pairs={{0,2},{2,0},{1,3},{3,1},{4,6},{6,4},{5,7},{7,5},{8,10},{10,8},{9,1... | collective-permute-start | bytes 7077896 | tf_op jit(solution)/shard_map/ppermute | solution.py:19
  5.9 4.3 %collective-permute-done.1 = f32[2,192,1536]{2,1,0:T(8,128)} collective-permute-done((f32[2,192,1536]{2,1,0:T(8,128)S(1)}, f32[2,192,1536]{2,1,0:T(8,128)}, u32[]{:S(2)}, u32[]{:S(2)}) %collective-permute-start.1) | collective-permute-done | bytes 2359328 | tf_op jit(solution)/shard_map/ppermute | solution.py:19
  10.1 2.8 %bitcast_add_fusion = f32[2,192,1536]{2,1,0:T(8,128)S(1)} fusion(f32[2,192,1536]{2,1,0:T(8,128)} %collective-permute-done.1, f32[1,4,192,1536]{3,2,1,0:T(8,128)} %param.5, s32[]{:T(128)S(6)} %select_n.129), kind=kLoop, calls=%fused_computation.7 | loop fusion | flops 589824 | bytes 7077892 | tf_op jit(solution)/shard_map/add | solution.py:65
  12.9 1.2 dynamic-slice_bitcast_fusion.3
  14.1 1.0 collective-permute-start.4
  15.1 0.3 collective-permute-start.3
  15.4 0.7 collective-permute-start.2
  16.1 12.8 %collective-permute-done.4 = f32[384,384]{0,1:T(8,128)} collective-permute-done((f32[384,384]{0,1:T(8,128)}, f32[384,384]{0,1:T(8,128)}, u32[]{:S(2)}, u32[]{:S(2)}) %collective-permute-start.4) | collective-permute-done | bytes 589856 | tf_op jit(solution)/shard_map/ppermute | solution.py:14
  28.9 2.3 %collective-permute-done.3 = f32[384,384]{0,1:T(8,128)} collective-permute-done((f32[384,384]{0,1:T(8,128)}, f32[384,384]{0,1:T(8,128)}, u32[]{:S(2)}, u32[]{:S(2)}) %collective-permute-start.3) | collective-permute-done | bytes 589856 | tf_op jit(solution)/shard_map/ppermute | solution.py:14
  31.2 13.3 %collective-permute-done.2 = f32[384,384]{0,1:T(8,128)} collective-permute-done((f32[384,384]{0,1:T(8,128)S(1)}, f32[384,384]{0,1:T(8,128)}, u32[]{:S(2)}, u32[]{:S(2)}) %collective-permute-start.2) | collective-permute-done | bytes 589856 | tf_op jit(solution)/shard_map/ppermute | solution.py:14
  44.5 1.5 fusion.4
  46.0 0.2 constant_dynamic-slice_fusion
  46.2 2.8 %collective-permute-start.5 = (f32[192,384]{0,1:T(8,128)S(1)}, f32[192,384]{0,1:T(8,128)S(1)}, u32[]{:S(2)}, u32[]{:S(2)}) collective-permute-start(f32[192,384]{0,1:T(8,128)S(1)} %constant_dynamic-slice_fusion), channel_id=1, source_target_pairs={{0,4},{4,0},{1,5},{5,1},{2,6},{6,2},{3,7},{7,3},{8,12},{12,8},{9,1... | collective-permute-start | bytes 884744 | tf_op jit(solution)/shard_map/ppermute | solution.py:14
  49.0 1.1 constant_dynamic-slice_fusion.1
  50.3 7.6 %collective-permute-done.5 = f32[192,384]{0,1:T(8,128)S(1)} collective-permute-done((f32[192,384]{0,1:T(8,128)S(1)}, f32[192,384]{0,1:T(8,128)S(1)}, u32[]{:S(2)}, u32[]{:S(2)}) %collective-permute-start.5) | collective-permute-done | bytes 294944 | tf_op jit(solution)/shard_map/ppermute | solution.py:14
  57.8 0.2 dynamic-slice_add_fusion
  58.0 0.9 copy.21
  58.9 8.2 %all-to-all-start = ((f32[8,24,384]{2,1,0:T(8,128)}), f32[8,24,384]{2,1,0:T(8,128)S(1)}, u32[]{:S(2)}, u32[]{:S(2)}) async-start(f32[8,24,384]{2,1,0:T(8,128)} %bitcast.9), calls=%async_computation | async-start | bytes 589824 | tf_op jit(solution)/shard_map/all_to_all | solution.py:53
  67.1 1.2 collective-permute-start
  68.4 1.5 collective-permute-done
  70.0 7.4 %all-to-all-done = f32[8,24,384]{2,1,0:T(8,128)S(1)} async-done(((f32[8,24,384]{2,1,0:T(8,128)}), f32[8,24,384]{2,1,0:T(8,128)S(1)}, u32[]{:S(2)}, u32[]{:S(2)}) %all-to-all-start) | async-done | bytes 294944 | tf_op jit(solution)/shard_map/all_to_all | solution.py:53
  77.4 0.1 reshape.43
  77.5 0.3 fusion.5
  77.8 1.3 collective-permute-start.6
  79.1 1.4 collective-permute-done.6
  80.5 0.1 fusion.20
  80.8 18.8 %all_gather.6 = f32[192,384]{1,0:T(8,128)S(1)} all-gather(f32[24,384]{1,0:T(8,128)S(1)} %pad_maximum_fusion.3), channel_id=1, replica_groups=mesh['z'=8,'y'=4,'xh'=2,'core'=2,'xl'=2] {'z'}, dimensions={0}, use_global_device_ids=true | all-gather | bytes 331776 | tf_op jit(solution)/shard_map/all_gather | solution.py:106
  99.6 2.7 %collective-permute-start.7 = (f32[192,384]{1,0:T(8,128)S(1)}, f32[192,384]{1,0:T(8,128)S(1)}, u32[]{:S(2)}, u32[]{:S(2)}) collective-permute-start(f32[192,384]{1,0:T(8,128)S(1)} %all_gather.6), channel_id=1, source_target_pairs={{0,4},{4,0},{1,5},{5,1},{2,6},{6,2},{3,7},{7,3},{8,12},{12,8},{9,1... | collective-permute-start | bytes 884744 | tf_op jit(solution)/shard_map/ppermute | solution.py:14
  102.3 0.2 copy.23
  102.5 3.5 %dynamic_update_slice.18 = f32[384,384]{0,1:T(8,128)S(1)} dynamic-update-slice(f32[384,384]{0,1:T(8,128)S(1)} %broadcast_in_dim.15, f32[192,384]{0,1:T(8,128)S(1)} %copy.23, s32[]{:T(128)S(6)} %select_n.141, s32[]{:T(128)} %constant.94.clone.1) | dynamic-update-slice | bytes 589828 | tf_op jit(solution)/shard_map/dynamic_update_slice | solution.py:44
  106.0 0.6 collective-permute-done.7
  106.6 0.2 copy.24
  106.8 3.4 %dynamic_update_slice.19 = f32[384,384]{0,1:T(8,128)S(1)} dynamic-update-slice(f32[384,384]{0,1:T(8,128)S(1)} %dynamic_update_slice.18, f32[192,384]{0,1:T(8,128)S(1)} %copy.24, s32[]{:T(128)S(6)} %select_n.147, s32[]{:T(128)} %constant.94.clone.1) | dynamic-update-slice | bytes 589828 | tf_op jit(solution)/shard_map/dynamic_update_slice | solution.py:46
  110.3 1.3 collective-permute-start.9
  111.6 2.0 collective-permute-start.10
  113.6 0.3 broadcast_in_dim.14
  114.0 13.3 %collective-permute-done.8 = f32[384,384]{0,1:T(8,128)} collective-permute-done((f32[384,384]{0,1:T(8,128)S(1)}, f32[384,384]{0,1:T(8,128)}, u32[]{:S(2)}, u32[]{:S(2)}) %collective-permute-start.8) | collective-permute-done | bytes 589856 | tf_op jit(solution)/shard_map/ppermute | solution.py:14
  127.2 1.1 constant_dynamic-update-slice_fusion.2
  128.4 1.1 constant_dynamic-update-slice_fusion.1
  129.5 1.1 constant_dynamic-update-slice_fusion
  130.7 13.0 %collective-permute-start.11 = (f32[1536,384]{0,1:T(8,128)S(1)}, f32[1536,384]{0,1:T(8,128)}, u32[]{:S(2)}, u32[]{:S(2)}) collective-permute-start(f32[1536,384]{0,1:T(8,128)S(1)} %constant_dynamic-update-slice_fusion), channel_id=1, source_target_pairs={{0,2},{2,0},{1,3},{3,1},{4,6},{6,4},{5,7},{7,5},{8,10},{10,8},{9,1... | collective-permute-start | bytes 7077896 | tf_op jit(solution)/shard_map/ppermute | solution.py:19
  143.7 0.5 fusion.13
  144.2 13.6 %all_to_all.10 = f32[8,48,128]{2,1,0:T(8,128)S(1)} all-to-all(f32[8,48,128]{2,1,0:T(8,128)S(1)} %bitcast.53), channel_id=1, replica_groups=mesh['z'=8,'y'=4,'xh'=2,'core'=2,'xl'=2] {'z'}, dimensions={0} | all-to-all | bytes 393216 | tf_op jit(solution)/shard_map/all_to_all | solution.py:53
  157.9 2.7 %collective-permute-done.12 = f32[48,128]{1,0:T(8,128)S(1)} collective-permute-done((f32[48,128]{1,0:T(8,128)S(1)}, f32[48,128]{1,0:T(8,128)S(1)}, u32[]{:S(2)}, u32[]{:S(2)}) %collective-permute-start.12) | collective-permute-done | bytes 24608 | tf_op jit(solution)/shard_map/ppermute | solution.py:19
  160.6 0.3 collective-permute-start.13
  160.8 3.9 %collective-permute-done.13 = f32[48,128]{1,0:T(8,128)S(1)} collective-permute-done((f32[48,128]{1,0:T(8,128)S(1)}, f32[48,128]{1,0:T(8,128)S(1)}, u32[]{:S(2)}, u32[]{:S(2)}) %collective-permute-start.13) | collective-permute-done | bytes 24608 | tf_op jit(solution)/shard_map/ppermute | solution.py:19
  164.7 2.8 %collective-permute-start.14 = (f32[48,128]{1,0:T(8,128)S(1)}, f32[48,128]{1,0:T(8,128)S(1)}, u32[]{:S(2)}, u32[]{:S(2)}) collective-permute-start(f32[48,128]{1,0:T(8,128)S(1)} %add.190), channel_id=1, source_target_pairs={{0,4},{4,0},{1,5},{5,1},{2,6},{6,2},{3,7},{7,3},{8,12},{12,8},{9,1... | collective-permute-start | bytes 73736 | tf_op jit(solution)/shard_map/ppermute | solution.py:19
  167.6 1.4 collective-permute-done.14
  168.9 18.6 %all_gather.7 = f32[384,128]{1,0:T(8,128)S(1)} all-gather(f32[48,128]{1,0:T(8,128)S(1)} %add.191), channel_id=1, replica_groups=mesh['z'=8,'y'=4,'xh'=2,'core'=2,'xl'=2] {'z'}, dimensions={0}, use_global_device_ids=true | all-gather | bytes 221184 | tf_op jit(solution)/shard_map/all_gather | solution.py:97
  187.6 0.7 fusion.27
  188.2 1.3 collective-permute-start.15
  189.6 2.9 %collective-permute-done.15 = f32[2,128,128]{2,1,0:T(8,128)S(1)} collective-permute-done((f32[2,128,128]{2,1,0:T(8,128)S(1)}, f32[2,128,128]{2,1,0:T(8,128)S(1)}, u32[]{:S(2)}, u32[]{:S(2)}) %collective-permute-start.15) | collective-permute-done | bytes 131104 | tf_op jit(solution)/shard_map/ppermute | solution.py:19
  192.4 0.1 select_reduce_fusion
  192.6 0.4 multiply_subtract_fusion
  193.0 11.1 %collective-permute-start.16 = (f32[2,192,128]{2,1,0:T(8,128)S(1)}, f32[2,192,128]{2,1,0:T(8,128)S(1)}, u32[]{:S(2)}, u32[]{:S(2)}) collective-permute-start(f32[2,192,128]{2,1,0:T(8,128)S(1)} %multiply_subtract_fusion), channel_id=1, source_target_pairs={{0,2},{2,0},{1,3},{3,1},{4,6},{6,4},{5,7},{7,5},{8,10},{10,8},{9,1... | collective-permute-start | bytes 589832 | tf_op jit(solution)/shard_map/ppermute | solution.py:19
  204.1 1.1 collective-permute-done.16
  205.2 0.8 pad_maximum_fusion.2
  206.0 2.1 select_bitcast_fusion
  208.1 1.7 pad_maximum_fusion.1
  209.8 0.3 pad_maximum_fusion
  210.1 2.4 %copy.25 = f32[2,3072,128]{2,1,0:T(8,128)} copy(f32[2,3072,128]{1,2,0:T(8,128)S(1)} %pad_maximum_fusion) | data formatting | bytes 6291456 | tf_op jit(solution)/shard_map/concatenate
  212.4 4.9 %fusion = (f32[4,64,1536]{2,1,0:T(8,128)}, f32[4,64,1536]{2,1,0:T(8,128)}) fusion(f32[4,64,1536]{2,1,0:T(8,128)} %bitcast.50, f32[4,64,1536]{2,1,0:T(8,128)} %param.9, f32[4,64,1536]{2,1,0:T(8,128)} %param.8), kind=kLoop, calls=%fused_computation.11 | loop fusion | flops 2752512 | bytes 7864320 | tf_op jit(solution)/shard_map/add | solution.py:114
  217.3 7.3 %bitcast_subtract_fusion = f32[4,192,1536]{2,1,0:T(8,128)} fusion(f32[4,192,1536]{2,1,0:T(8,128)} %param.7, f32[4,1536,128]{2,1,0:T(8,128)S(1)} %bitcast.47, f32[4,192,128]{2,1,0:T(8,128)S(1)} %copy-done), kind=kOutput, calls=%fused_computation.4 | convolution fusion | flops 1814298624 | bytes 12976128 | tf_op jit(solution)/shard_map/ldr,lfr->ldf/dot_general | solution.py:116
  (29 shorter events, 1.0 us)
Async XLA Ops:
  0.6 76.8 %copy-start = (f32[4,192,128]{2,1,0:T(8,128)S(1)}, f32[4,192,128]{2,1,0:T(8,128)}, u32[]{:S(2)}) copy-start(f32[4,192,128]{2,1,0:T(8,128)} %param.6) | copy-start | bytes 1179652
  2.5 7.6 %collective-permute-start.1 = (f32[2,192,1536]{2,1,0:T(8,128)S(1)}, f32[2,192,1536]{2,1,0:T(8,128)}, u32[]{:S(2)}, u32[]{:S(2)}) collective-permute-start(f32[2,192,1536]{2,1,0:T(8,128)S(1)} %dynamic-slice_bitcast_fusion), channel_id=1, source_target_pairs={{0,2},{2,0},{1,3},{3,1},{4,6},{6,4},{5,7},{7,5},{8,10},{10,8},{9,1... | collective-permute-start | bytes 7077896 | tf_op jit(solution)/shard_map/ppermute | solution.py:19
  14.1 14.9 %collective-permute-start.4 = (f32[384,384]{0,1:T(8,128)}, f32[384,384]{0,1:T(8,128)}, u32[]{:S(2)}, u32[]{:S(2)}) collective-permute-start(f32[384,384]{0,1:T(8,128)} %get-tuple-element.16), channel_id=1, source_target_pairs={{0,24},{8,0},{16,8},{24,16},{1,25},{9,1},{17,9},{25,17},{2,26},{10... | collective-permute-start | bytes 1769480 | tf_op jit(solution)/shard_map/ppermute | solution.py:14
  15.1 16.1 %collective-permute-start.3 = (f32[384,384]{0,1:T(8,128)}, f32[384,384]{0,1:T(8,128)}, u32[]{:S(2)}, u32[]{:S(2)}) collective-permute-start(f32[384,384]{0,1:T(8,128)} %get-tuple-element.17), channel_id=1, source_target_pairs={{0,16},{8,24},{16,0},{24,8},{1,17},{9,25},{17,1},{25,9},{2,18},{10... | collective-permute-start | bytes 1769480 | tf_op jit(solution)/shard_map/ppermute | solution.py:14
  15.4 29.0 %collective-permute-start.2 = (f32[384,384]{0,1:T(8,128)S(1)}, f32[384,384]{0,1:T(8,128)}, u32[]{:S(2)}, u32[]{:S(2)}) collective-permute-start(f32[384,384]{0,1:T(8,128)S(1)} %get-tuple-element.15), channel_id=1, source_target_pairs={{0,8},{8,16},{16,24},{24,0},{1,9},{9,17},{17,25},{25,1},{2,10},{10... | collective-permute-start | bytes 1769480 | tf_op jit(solution)/shard_map/ppermute | solution.py:14
  46.2 11.6 %collective-permute-start.5 = (f32[192,384]{0,1:T(8,128)S(1)}, f32[192,384]{0,1:T(8,128)S(1)}, u32[]{:S(2)}, u32[]{:S(2)}) collective-permute-start(f32[192,384]{0,1:T(8,128)S(1)} %constant_dynamic-slice_fusion), channel_id=1, source_target_pairs={{0,4},{4,0},{1,5},{5,1},{2,6},{6,2},{3,7},{7,3},{8,12},{12,8},{9,1... | collective-permute-start | bytes 884744 | tf_op jit(solution)/shard_map/ppermute | solution.py:14
  58.9 18.5 %all-to-all-start = ((f32[8,24,384]{2,1,0:T(8,128)}), f32[8,24,384]{2,1,0:T(8,128)S(1)}, u32[]{:S(2)}, u32[]{:S(2)}) async-start(f32[8,24,384]{2,1,0:T(8,128)} %bitcast.9), calls=%async_computation | async-start | bytes 589824 | tf_op jit(solution)/shard_map/all_to_all | solution.py:53
  67.1 2.7 %collective-permute-start = (f32[2,24,128]{2,1,0:T(8,128)S(1)}, f32[2,24,128]{2,1,0:T(8,128)S(1)}, u32[]{:S(2)}, u32[]{:S(2)}) collective-permute-start(f32[2,24,128]{2,1,0:T(8,128)S(1)} %pad_maximum_fusion.4), channel_id=1, source_target_pairs={{0,1},{1,0},{2,3},{3,2},{4,5},{5,4},{6,7},{7,6},{8,9},{9,8},{10,11... | collective-permute-start | bytes 73736 | tf_op jit(solution)/shard_map/ppermute | solution.py:19
  77.8 2.8 %collective-permute-start.6 = (f32[2,24,128]{2,1,0:T(8,128)S(1)}, f32[2,24,128]{2,1,0:T(8,128)S(1)}, u32[]{:S(2)}, u32[]{:S(2)}) collective-permute-start(f32[2,24,128]{2,1,0:T(8,128)S(1)} %fusion.5), channel_id=1, source_target_pairs={{0,1},{1,0},{2,3},{3,2},{4,5},{5,4},{6,7},{7,6},{8,9},{9,8},{10,11... | collective-permute-start | bytes 73736 | tf_op jit(solution)/shard_map/ppermute | solution.py:19
  99.6 7.1 %collective-permute-start.7 = (f32[192,384]{1,0:T(8,128)S(1)}, f32[192,384]{1,0:T(8,128)S(1)}, u32[]{:S(2)}, u32[]{:S(2)}) collective-permute-start(f32[192,384]{1,0:T(8,128)S(1)} %all_gather.6), channel_id=1, source_target_pairs={{0,4},{4,0},{1,5},{5,1},{2,6},{6,2},{3,7},{7,3},{8,12},{12,8},{9,1... | collective-permute-start | bytes 884744 | tf_op jit(solution)/shard_map/ppermute | solution.py:14
  110.2 17.0 %collective-permute-start.8 = (f32[384,384]{0,1:T(8,128)S(1)}, f32[384,384]{0,1:T(8,128)}, u32[]{:S(2)}, u32[]{:S(2)}) collective-permute-start(f32[384,384]{0,1:T(8,128)S(1)} %dynamic_update_slice.19), channel_id=1, source_target_pairs={{0,8},{8,16},{16,24},{24,0},{1,9},{9,17},{17,25},{25,1},{2,10},{10... | collective-permute-start | bytes 1769480 | tf_op jit(solution)/shard_map/ppermute | solution.py:14
  110.3 18.1 %collective-permute-start.9 = (f32[384,384]{0,1:T(8,128)S(1)}, f32[384,384]{0,1:T(8,128)}, u32[]{:S(2)}, u32[]{:S(2)}) collective-permute-start(f32[384,384]{0,1:T(8,128)S(1)} %dynamic_update_slice.19), channel_id=1, source_target_pairs={{0,16},{8,24},{16,0},{24,8},{1,17},{9,25},{17,1},{25,9},{2,18},{10... | collective-permute-start | bytes 1769480 | tf_op jit(solution)/shard_map/ppermute | solution.py:14
  111.6 17.9 %collective-permute-start.10 = (f32[384,384]{0,1:T(8,128)S(1)}, f32[384,384]{0,1:T(8,128)}, u32[]{:S(2)}, u32[]{:S(2)}) collective-permute-start(f32[384,384]{0,1:T(8,128)S(1)} %dynamic_update_slice.19), channel_id=1, source_target_pairs={{0,24},{8,0},{16,8},{24,16},{1,25},{9,1},{17,9},{25,17},{2,26},{10... | collective-permute-start | bytes 1769480 | tf_op jit(solution)/shard_map/ppermute | solution.py:14
  130.7 75.3 %collective-permute-start.11 = (f32[1536,384]{0,1:T(8,128)S(1)}, f32[1536,384]{0,1:T(8,128)}, u32[]{:S(2)}, u32[]{:S(2)}) collective-permute-start(f32[1536,384]{0,1:T(8,128)S(1)} %constant_dynamic-update-slice_fusion), channel_id=1, source_target_pairs={{0,2},{2,0},{1,3},{3,1},{4,6},{6,4},{5,7},{7,5},{8,10},{10,8},{9,1... | collective-permute-start | bytes 7077896 | tf_op jit(solution)/shard_map/ppermute | solution.py:19
  157.8 2.8 %collective-permute-start.12 = (f32[48,128]{1,0:T(8,128)S(1)}, f32[48,128]{1,0:T(8,128)S(1)}, u32[]{:S(2)}, u32[]{:S(2)}) collective-permute-start(f32[48,128]{1,0:T(8,128)S(1)} %reduce_sum.28), channel_id=1, source_target_pairs={{0,8},{8,0},{16,24},{24,16},{1,9},{9,1},{17,25},{25,17},{2,10},{10... | collective-permute-start | bytes 73736 | tf_op jit(solution)/shard_map/ppermute | solution.py:19
  160.6 4.2 %collective-permute-start.13 = (f32[48,128]{1,0:T(8,128)S(1)}, f32[48,128]{1,0:T(8,128)S(1)}, u32[]{:S(2)}, u32[]{:S(2)}) collective-permute-start(f32[48,128]{1,0:T(8,128)S(1)} %add.189), channel_id=1, source_target_pairs={{0,16},{8,24},{16,0},{24,8},{1,17},{9,25},{17,1},{25,9},{2,18},{10... | collective-permute-start | bytes 73736 | tf_op jit(solution)/shard_map/ppermute | solution.py:19
  164.7 4.2 %collective-permute-start.14 = (f32[48,128]{1,0:T(8,128)S(1)}, f32[48,128]{1,0:T(8,128)S(1)}, u32[]{:S(2)}, u32[]{:S(2)}) collective-permute-start(f32[48,128]{1,0:T(8,128)S(1)} %add.190), channel_id=1, source_target_pairs={{0,4},{4,0},{1,5},{5,1},{2,6},{6,2},{3,7},{7,3},{8,12},{12,8},{9,1... | collective-permute-start | bytes 73736 | tf_op jit(solution)/shard_map/ppermute | solution.py:19
  188.2 4.2 %collective-permute-start.15 = (f32[2,128,128]{2,1,0:T(8,128)S(1)}, f32[2,128,128]{2,1,0:T(8,128)S(1)}, u32[]{:S(2)}, u32[]{:S(2)}) collective-permute-start(f32[2,128,128]{2,1,0:T(8,128)S(1)} %fusion.27), channel_id=1, source_target_pairs={{0,1},{1,0},{2,3},{3,2},{4,5},{5,4},{6,7},{7,6},{8,9},{9,8},{10,11... | collective-permute-start | bytes 393224 | tf_op jit(solution)/shard_map/ppermute | solution.py:19
  193.0 12.2 %collective-permute-start.16 = (f32[2,192,128]{2,1,0:T(8,128)S(1)}, f32[2,192,128]{2,1,0:T(8,128)S(1)}, u32[]{:S(2)}, u32[]{:S(2)}) collective-permute-start(f32[2,192,128]{2,1,0:T(8,128)S(1)} %multiply_subtract_fusion), channel_id=1, source_target_pairs={{0,2},{2,0},{1,3},{3,1},{4,6},{6,4},{5,7},{7,5},{8,10},{10,8},{9,1... | collective-permute-start | bytes 589832 | tf_op jit(solution)/shard_map/ppermute | solution.py:19
  212.4 4.9 %copy-start.1 = (f32[2,3072,128]{2,1,0:T(8,128)S(1)}, f32[2,3072,128]{2,1,0:T(8,128)}, u32[]{:S(2)}) copy-start(f32[2,3072,128]{2,1,0:T(8,128)} %copy.25) | copy-start | bytes 9437188
where the time goes:
time: 225 us
  waiting for transfers between devices  76.2 us (34%)
  starting transfers between devices  53.7 us (24%)
  blocking collectives  51 us (23%)
  local copies, waits for them, and re-layouts  18.9 us (8%)
  other arithmetic  14.8 us (7%)
  matrix products  9.18 us (4%)
    ppermute x8, waiting for transfers between devices, shift(): return lax.ppermute(x, axis, [(i, (i + k) % n) for i in range(n)])  49.8 us
    ppermute x9, starting transfers between devices, flip(): return lax.ppermute(x, axis, [(i, i ^ bit) for i in range(n)])  34.5 us
    ppermute x9, waiting for transfers between devices, flip(): return lax.ppermute(x, axis, [(i, i ^ bit) for i in range(n)])  19 us
    all_gather x1, blocking collectives, on_device(): packed = lax.all_gather(packed, 'z', axis=0, tiled=True)  18.8 us
    all_gather x1, blocking collectives, on_device(): lax.all_gather(part, 'z', axis=0, tiled=True).reshape(half, depth, rank)  18.6 us
    all_to_all x1, blocking collectives, scatter_exchange(): lax.all_to_all(parts, axis, split_axis=0, concat_axis=0)  13.6 us
    ppermute x8, starting transfers between devices, shift(): return lax.ppermute(x, axis, [(i, (i + k) % n) for i in range(n)])  11 us
    all_to_all x1, starting transfers between devices, scatter_exchange(): lax.all_to_all(parts, axis, split_axis=0, concat_axis=0)  8.19 us
  transfers between devices with their start and end apart: 18, of which 15 were waited for; matrix products, arithmetic and copies ran while one was open for 5% of the time, Pallas kernels for 0%

commit v1 on v0

--- a/solution.py
+++ b/solution.py
@@ -94,7 +94,9 @@
     part = part + flip(part, "y", 1)
     part = part + flip(part, "y", 2)
     part = part + flip(part, "xh")
-    refresh = lax.all_gather(part, "z", axis=0, tiled=True).reshape(half, depth, rank)
+    refresh = jnp.concatenate(
+        lax.all_to_all(jnp.stack([part] * lax.axis_size("z")), "z", 0, 0), axis=0
+    ).reshape(half, depth, rank)
     gram = jnp.einsum("ldr,lds->lrs", refresh, refresh, precision=HIGH)
     gram = gram + flip(gram, "xl")
     sumsq = jnp.einsum("lrr->l", gram)

time: 225 us -> 199 us (0.88)
  blocking collectives: 51 us -> 30.3 us
  waiting for transfers between devices: 76.2 us -> 70.9 us
    all_gather x1 -> x0, blocking collectives: 18.6 us -> none  [on_device(): lax.all_gather(part, 'z', axis=0, tiled=True).reshape(half, depth, rank)]
    ppermute x9, starting transfers between devices: 34.5 us -> 29.9 us  [flip(): return lax.ppermute(x, axis, [(i, i ^ bit) for i in range(n)])]
    ppermute x8, waiting for transfers between devices: 49.8 us -> 45.2 us  [shift(): return lax.ppermute(x, axis, [(i, (i + k) % n) for i in range(n)])]
    all_to_all x1 -> x2, starting transfers between devices: 8.19 us -> 11.6 us  [scatter_exchange(): lax.all_to_all(parts, axis, split_axis=0, concat_axis=0)]
    all_to_all x1 -> x2, waiting for transfers between devices: 7.36 us -> 7.36 us  [scatter_exchange(): lax.all_to_all(parts, axis, split_axis=0, concat_axis=0)]
  transfers between devices with their start and end apart: 18 -> 19, of which waited for: 15 -> 15; matrix products, arithmetic and copies ran while one was open for 5% -> 6% of each run, Pallas kernels for 0% -> 0%
where the time goes in v1:
time: 199 us; the launch traced here: 198 us
  waiting for transfers between devices  70.9 us (36%)
  starting transfers between devices  52.4 us (26%)
  blocking collectives  30.3 us (15%)
  local copies, waits for them, and re-layouts  18.9 us (9%)
  other arithmetic  14.8 us (7%)
  matrix products  9.87 us (5%)
    ppermute x8, waiting for transfers between devices, shift(): return lax.ppermute(x, axis, [(i, (i + k) % n) for i in range(n)])  45.2 us
    ppermute x9, starting transfers between devices, flip(): return lax.ppermute(x, axis, [(i, i ^ bit) for i in range(n)])  29.9 us
    all_gather x1, blocking collectives, on_device(): packed = lax.all_gather(packed, 'z', axis=0, tiled=True)  18.8 us
    ppermute x9, waiting for transfers between devices, flip(): return lax.ppermute(x, axis, [(i, i ^ bit) for i in range(n)])  18.3 us
    all_to_all x2, starting transfers between devices, scatter_exchange(): lax.all_to_all(parts, axis, split_axis=0, concat_axis=0)  11.6 us
    all_to_all x1, blocking collectives, on_device(): lax.all_to_all(jnp.stack([part] * lax.axis_size('z')), 'z', 0, 0)  11.5 us
    ppermute x8, starting transfers between devices, shift(): return lax.ppermute(x, axis, [(i, (i + k) % n) for i in range(n)])  11 us
    all_to_all x2, waiting for transfers between devices, scatter_exchange(): lax.all_to_all(parts, axis, split_axis=0, concat_axis=0)  7.36 us
  transfers between devices with their start and end apart: 19, of which 15 were waited for; matrix products, arithmetic and copies ran while one was open for 6% of the time, Pallas kernels for 0%

profile of v1, /device:TPU:1, one launch (start us, length us, event | category | flops | bytes accessed | tf_op | source)
XLA Modules:
  0.0 198.1 jit_solution(12746454700547666834)
XLA Ops:
  0.7 1.9 dynamic-slice_bitcast_fusion
  2.5 3.3 %collective-permute-start.1 = (f32[2,192,1536]{2,1,0:T(8,128)S(1)}, f32[2,192,1536]{2,1,0:T(8,128)}, u32[]{:S(2)}, u32[]{:S(2)}) collective-permute-start(f32[2,192,1536]{2,1,0:T(8,128)S(1)} %dynamic-slice_bitcast_fusion), channel_id=1, source_target_pairs={{0,2},{2,0},{1,3},{3,1},{4,6},{6,4},{5,7},{7,5},{8,10},{10,8},{9,1... | collective-permute-start | bytes 7077896 | tf_op jit(solution)/shard_map/ppermute | solution.py:19
  5.9 4.3 %collective-permute-done.1 = f32[2,192,1536]{2,1,0:T(8,128)} collective-permute-done((f32[2,192,1536]{2,1,0:T(8,128)S(1)}, f32[2,192,1536]{2,1,0:T(8,128)}, u32[]{:S(2)}, u32[]{:S(2)}) %collective-permute-start.1) | collective-permute-done | bytes 2359328 | tf_op jit(solution)/shard_map/ppermute | solution.py:19
  10.1 2.8 %bitcast_add_fusion = f32[2,192,1536]{2,1,0:T(8,128)S(1)} fusion(f32[2,192,1536]{2,1,0:T(8,128)} %collective-permute-done.1, f32[1,4,192,1536]{3,2,1,0:T(8,128)} %param.5, s32[]{:T(128)S(6)} %select_n.129), kind=kLoop, calls=%fused_computation.7 | loop fusion | flops 589824 | bytes 7077892 | tf_op jit(solution)/shard_map/add | solution.py:65
  12.9 1.2 dynamic-slice_bitcast_fusion.3
  14.1 1.0 collective-permute-start.4
  15.1 0.3 collective-permute-start.3
  15.4 0.7 collective-permute-start.2
  16.1 12.8 %collective-permute-done.4 = f32[384,384]{0,1:T(8,128)} collective-permute-done((f32[384,384]{0,1:T(8,128)}, f32[384,384]{0,1:T(8,128)}, u32[]{:S(2)}, u32[]{:S(2)}) %collective-permute-start.4) | collective-permute-done | bytes 589856 | tf_op jit(solution)/shard_map/ppermute | solution.py:14
  28.9 2.3 %collective-permute-done.3 = f32[384,384]{0,1:T(8,128)} collective-permute-done((f32[384,384]{0,1:T(8,128)}, f32[384,384]{0,1:T(8,128)}, u32[]{:S(2)}, u32[]{:S(2)}) %collective-permute-start.3) | collective-permute-done | bytes 589856 | tf_op jit(solution)/shard_map/ppermute | solution.py:14
  31.2 13.3 %collective-permute-done.2 = f32[384,384]{0,1:T(8,128)} collective-permute-done((f32[384,384]{0,1:T(8,128)S(1)}, f32[384,384]{0,1:T(8,128)}, u32[]{:S(2)}, u32[]{:S(2)}) %collective-permute-start.2) | collective-permute-done | bytes 589856 | tf_op jit(solution)/shard_map/ppermute | solution.py:14
  44.5 1.5 fusion.5
  46.0 0.2 constant_dynamic-slice_fusion
  46.2 2.8 %collective-permute-start.5 = (f32[192,384]{0,1:T(8,128)S(1)}, f32[192,384]{0,1:T(8,128)S(1)}, u32[]{:S(2)}, u32[]{:S(2)}) collective-permute-start(f32[192,384]{0,1:T(8,128)S(1)} %constant_dynamic-slice_fusion), channel_id=1, source_target_pairs={{0,4},{4,0},{1,5},{5,1},{2,6},{6,2},{3,7},{7,3},{8,12},{12,8},{9,1... | collective-permute-start | bytes 884744 | tf_op jit(solution)/shard_map/ppermute | solution.py:14
  49.0 1.1 constant_dynamic-slice_fusion.1
  50.3 7.6 %collective-permute-done.5 = f32[192,384]{0,1:T(8,128)S(1)} collective-permute-done((f32[192,384]{0,1:T(8,128)S(1)}, f32[192,384]{0,1:T(8,128)S(1)}, u32[]{:S(2)}, u32[]{:S(2)}) %collective-permute-start.5) | collective-permute-done | bytes 294944 | tf_op jit(solution)/shard_map/ppermute | solution.py:14
  57.8 0.2 dynamic-slice_add_fusion
  58.0 0.9 copy.21
  58.9 8.2 %all-to-all-start = ((f32[8,24,384]{2,1,0:T(8,128)}), f32[8,24,384]{2,1,0:T(8,128)S(1)}, u32[]{:S(2)}, u32[]{:S(2)}) async-start(f32[8,24,384]{2,1,0:T(8,128)} %bitcast.9), calls=%async_computation | async-start | bytes 589824 | tf_op jit(solution)/shard_map/all_to_all | solution.py:53
  67.1 1.2 collective-permute-start
  68.4 1.5 collective-permute-done
  70.0 7.4 %all-to-all-done = f32[8,24,384]{2,1,0:T(8,128)S(1)} async-done(((f32[8,24,384]{2,1,0:T(8,128)}), f32[8,24,384]{2,1,0:T(8,128)S(1)}, u32[]{:S(2)}, u32[]{:S(2)}) %all-to-all-start) | async-done | bytes 294944 | tf_op jit(solution)/shard_map/all_to_all | solution.py:53
  77.4 0.1 reshape.42
  77.5 0.3 fusion.7
  77.8 1.3 collective-permute-start.6
  79.1 1.4 collective-permute-done.6
  80.5 0.1 fusion.19
  80.8 18.8 %all_gather.3 = f32[192,384]{1,0:T(8,128)S(1)} all-gather(f32[24,384]{1,0:T(8,128)S(1)} %pad_maximum_fusion.3), channel_id=1, replica_groups=mesh['z'=8,'y'=4,'xh'=2,'core'=2,'xl'=2] {'z'}, dimensions={0}, use_global_device_ids=true | all-gather | bytes 331776 | tf_op jit(solution)/shard_map/all_gather | solution.py:108
  99.6 2.7 %collective-permute-start.7 = (f32[192,384]{1,0:T(8,128)S(1)}, f32[192,384]{1,0:T(8,128)S(1)}, u32[]{:S(2)}, u32[]{:S(2)}) collective-permute-start(f32[192,384]{1,0:T(8,128)S(1)} %all_gather.3), channel_id=1, source_target_pairs={{0,4},{4,0},{1,5},{5,1},{2,6},{6,2},{3,7},{7,3},{8,12},{12,8},{9,1... | collective-permute-start | bytes 884744 | tf_op jit(solution)/shard_map/ppermute | solution.py:14
  102.3 0.2 copy.23
  102.5 3.5 %dynamic_update_slice.18 = f32[384,384]{0,1:T(8,128)S(1)} dynamic-update-slice(f32[384,384]{0,1:T(8,128)S(1)} %broadcast_in_dim.15, f32[192,384]{0,1:T(8,128)S(1)} %copy.23, s32[]{:T(128)S(6)} %select_n.141, s32[]{:T(128)} %constant.94.clone.1) | dynamic-update-slice | bytes 589828 | tf_op jit(solution)/shard_map/dynamic_update_slice | solution.py:44
  106.0 0.6 collective-permute-done.7
  106.6 0.2 copy.24
  106.8 3.4 %dynamic_update_slice.19 = f32[384,384]{0,1:T(8,128)S(1)} dynamic-update-slice(f32[384,384]{0,1:T(8,128)S(1)} %dynamic_update_slice.18, f32[192,384]{0,1:T(8,128)S(1)} %copy.24, s32[]{:T(128)S(6)} %select_n.147, s32[]{:T(128)} %constant.94.clone.1) | dynamic-update-slice | bytes 589828 | tf_op jit(solution)/shard_map/dynamic_update_slice | solution.py:46
  110.3 1.3 collective-permute-start.9
  111.6 2.0 collective-permute-start.10
  113.6 1.2 fusion.12
  114.8 3.4 %all-to-all-start.1 = ((f32[8,48,128]{2,1,0:T(8,128)}), f32[8,48,128]{2,1,0:T(8,128)S(1)}, u32[]{:S(2)}, u32[]{:S(2)}) async-start(f32[8,48,128]{2,1,0:T(8,128)} %bitcast.23), calls=%async_computation.1 | async-start | bytes 393216 | tf_op jit(solution)/shard_map/all_to_all | solution.py:53
  118.2 0.3 broadcast_in_dim.14
  118.5 8.7 %collective-permute-done.8 = f32[384,384]{0,1:T(8,128)} collective-permute-done((f32[384,384]{0,1:T(8,128)S(1)}, f32[384,384]{0,1:T(8,128)}, u32[]{:S(2)}, u32[]{:S(2)}) %collective-permute-start.8) | collective-permute-done | bytes 589856 | tf_op jit(solution)/shard_map/ppermute | solution.py:14
  127.2 1.1 constant_dynamic-update-slice_fusion.2
  128.4 1.1 constant_dynamic-update-slice_fusion.1
  129.5 1.1 constant_dynamic-update-slice_fusion
  130.7 13.0 %collective-permute-start.11 = (f32[1536,384]{0,1:T(8,128)S(1)}, f32[1536,384]{0,1:T(8,128)}, u32[]{:S(2)}, u32[]{:S(2)}) collective-permute-start(f32[1536,384]{0,1:T(8,128)S(1)} %constant_dynamic-update-slice_fusion), channel_id=1, source_target_pairs={{0,2},{2,0},{1,3},{3,1},{4,6},{6,4},{5,7},{7,5},{8,10},{10,8},{9,1... | collective-permute-start | bytes 7077896 | tf_op jit(solution)/shard_map/ppermute | solution.py:19
  143.8 2.7 %collective-permute-done.12 = f32[48,128]{1,0:T(8,128)S(1)} collective-permute-done((f32[48,128]{1,0:T(8,128)S(1)}, f32[48,128]{1,0:T(8,128)S(1)}, u32[]{:S(2)}, u32[]{:S(2)}) %collective-permute-start.12) | collective-permute-done | bytes 24608 | tf_op jit(solution)/shard_map/ppermute | solution.py:19
  146.5 0.7 collective-permute-start.13
  147.2 3.4 %collective-permute-done.13 = f32[48,128]{1,0:T(8,128)S(1)} collective-permute-done((f32[48,128]{1,0:T(8,128)S(1)}, f32[48,128]{1,0:T(8,128)S(1)}, u32[]{:S(2)}, u32[]{:S(2)}) %collective-permute-start.13) | collective-permute-done | bytes 24608 | tf_op jit(solution)/shard_map/ppermute | solution.py:19
  150.7 2.8 %collective-permute-start.14 = (f32[48,128]{1,0:T(8,128)S(1)}, f32[48,128]{1,0:T(8,128)S(1)}, u32[]{:S(2)}, u32[]{:S(2)}) collective-permute-start(f32[48,128]{1,0:T(8,128)S(1)} %add.190), channel_id=1, source_target_pairs={{0,4},{4,0},{1,5},{5,1},{2,6},{6,2},{3,7},{7,3},{8,12},{12,8},{9,1... | collective-permute-start | bytes 73736 | tf_op jit(solution)/shard_map/ppermute | solution.py:19
  153.5 1.4 collective-permute-done.14
  154.9 11.5 %all_to_all.15 = f32[8,48,128]{2,1,0:T(8,128)S(1)} all-to-all(f32[8,48,128]{2,1,0:T(8,128)S(1)} %stack.11), channel_id=1, replica_groups=mesh['z'=8,'y'=4,'xh'=2,'core'=2,'xl'=2] {'z'}, dimensions={0} | all-to-all | bytes 393216 | tf_op jit(solution)/shard_map/all_to_all | solution.py:98
  166.4 0.7 fusion.26
  167.1 1.3 collective-permute-start.15
  168.4 2.6 %collective-permute-done.15 = f32[2,128,128]{2,1,0:T(8,128)S(1)} collective-permute-done((f32[2,128,128]{2,1,0:T(8,128)S(1)}, f32[2,128,128]{2,1,0:T(8,128)S(1)}, u32[]{:S(2)}, u32[]{:S(2)}) %collective-permute-start.15) | collective-permute-done | bytes 131104 | tf_op jit(solution)/shard_map/ppermute | solution.py:19
  171.0 0.1 select_reduce_fusion
  171.1 0.4 fusion.3
  171.5 6.0 %collective-permute-start.16 = (f32[2,192,128]{2,1,0:T(8,128)S(1)}, f32[2,192,128]{2,1,0:T(8,128)S(1)}, u32[]{:S(2)}, u32[]{:S(2)}) collective-permute-start(f32[2,192,128]{2,1,0:T(8,128)S(1)} %fusion.3), channel_id=1, source_target_pairs={{0,2},{2,0},{1,3},{3,1},{4,6},{6,4},{5,7},{7,5},{8,10},{10,8},{9,1... | collective-permute-start | bytes 589832 | tf_op jit(solution)/shard_map/ppermute | solution.py:19
  177.6 1.1 collective-permute-done.16
  178.7 0.8 pad_maximum_fusion.2
  179.5 2.1 %select_bitcast_fusion = (f32[1,1536,384]{1,2,0:T(8,128)S(1)}, f32[1,1536,384]{1,2,0:T(8,128)S(1)}) fusion(f32[1536,384]{0,1:T(8,128)} %collective-permute-done.11, f32[1536,384]{0,1:T(8,128)S(1)} %constant_dynamic-update-slice_fusion, pred[]{:T(512)S(6)} %eq.20), kind=kLoop, calls=%fused_computation.8 | loop fusion | flops 1179648 | bytes 9437185 | tf_op jit(solution)/shard_map/stack | solution.py:111
  181.6 1.7 pad_maximum_fusion.1
  183.3 0.3 pad_maximum_fusion
  183.5 2.4 %copy.25 = f32[2,3072,128]{2,1,0:T(8,128)} copy(f32[2,3072,128]{1,2,0:T(8,128)S(1)} %pad_maximum_fusion) | data formatting | bytes 6291456 | tf_op jit(solution)/shard_map/concatenate
  185.9 4.9 %fusion = (f32[4,64,1536]{2,1,0:T(8,128)}, f32[4,64,1536]{2,1,0:T(8,128)}) fusion(f32[4,64,1536]{2,1,0:T(8,128)} %bitcast.50, f32[4,64,1536]{2,1,0:T(8,128)} %param.9, f32[4,64,1536]{2,1,0:T(8,128)} %param.8), kind=kLoop, calls=%fused_computation.11 | loop fusion | flops 2752512 | bytes 7864320 | tf_op jit(solution)/shard_map/add | solution.py:116
  190.8 7.3 %bitcast_subtract_fusion = f32[4,192,1536]{2,1,0:T(8,128)} fusion(f32[4,192,1536]{2,1,0:T(8,128)} %param.7, f32[4,1536,128]{2,1,0:T(8,128)S(1)} %bitcast.47, f32[4,192,128]{2,1,0:T(8,128)S(1)} %copy-done), kind=kOutput, calls=%fused_computation.4 | convolution fusion | flops 1814298624 | bytes 12976128 | tf_op jit(solution)/shard_map/ldr,lfr->ldf/dot_general | solution.py:118
  (31 shorter events, 1.0 us)
Async XLA Ops:
  0.6 76.8 %copy-start = (f32[4,192,128]{2,1,0:T(8,128)S(1)}, f32[4,192,128]{2,1,0:T(8,128)}, u32[]{:S(2)}) copy-start(f32[4,192,128]{2,1,0:T(8,128)} %param.6) | copy-start | bytes 1179652
  2.5 7.6 %collective-permute-start.1 = (f32[2,192,1536]{2,1,0:T(8,128)S(1)}, f32[2,192,1536]{2,1,0:T(8,128)}, u32[]{:S(2)}, u32[]{:S(2)}) collective-permute-start(f32[2,192,1536]{2,1,0:T(8,128)S(1)} %dynamic-slice_bitcast_fusion), channel_id=1, source_target_pairs={{0,2},{2,0},{1,3},{3,1},{4,6},{6,4},{5,7},{7,5},{8,10},{10,8},{9,1... | collective-permute-start | bytes 7077896 | tf_op jit(solution)/shard_map/ppermute | solution.py:19
  14.1 14.9 %collective-permute-start.4 = (f32[384,384]{0,1:T(8,128)}, f32[384,384]{0,1:T(8,128)}, u32[]{:S(2)}, u32[]{:S(2)}) collective-permute-start(f32[384,384]{0,1:T(8,128)} %get-tuple-element.16), channel_id=1, source_target_pairs={{0,24},{8,0},{16,8},{24,16},{1,25},{9,1},{17,9},{25,17},{2,26},{10... | collective-permute-start | bytes 1769480 | tf_op jit(solution)/shard_map/ppermute | solution.py:14
  15.1 16.1 %collective-permute-start.3 = (f32[384,384]{0,1:T(8,128)}, f32[384,384]{0,1:T(8,128)}, u32[]{:S(2)}, u32[]{:S(2)}) collective-permute-start(f32[384,384]{0,1:T(8,128)} %get-tuple-element.17), channel_id=1, source_target_pairs={{0,16},{8,24},{16,0},{24,8},{1,17},{9,25},{17,1},{25,9},{2,18},{10... | collective-permute-start | bytes 1769480 | tf_op jit(solution)/shard_map/ppermute | solution.py:14
  15.4 29.0 %collective-permute-start.2 = (f32[384,384]{0,1:T(8,128)S(1)}, f32[384,384]{0,1:T(8,128)}, u32[]{:S(2)}, u32[]{:S(2)}) collective-permute-start(f32[384,384]{0,1:T(8,128)S(1)} %get-tuple-element.15), channel_id=1, source_target_pairs={{0,8},{8,16},{16,24},{24,0},{1,9},{9,17},{17,25},{25,1},{2,10},{10... | collective-permute-start | bytes 1769480 | tf_op jit(solution)/shard_map/ppermute | solution.py:14
  46.2 11.6 %collective-permute-start.5 = (f32[192,384]{0,1:T(8,128)S(1)}, f32[192,384]{0,1:T(8,128)S(1)}, u32[]{:S(2)}, u32[]{:S(2)}) collective-permute-start(f32[192,384]{0,1:T(8,128)S(1)} %constant_dynamic-slice_fusion), channel_id=1, source_target_pairs={{0,4},{4,0},{1,5},{5,1},{2,6},{6,2},{3,7},{7,3},{8,12},{12,8},{9,1... | collective-permute-start | bytes 884744 | tf_op jit(solution)/shard_map/ppermute | solution.py:14
  58.9 18.5 %all-to-all-start = ((f32[8,24,384]{2,1,0:T(8,128)}), f32[8,24,384]{2,1,0:T(8,128)S(1)}, u32[]{:S(2)}, u32[]{:S(2)}) async-start(f32[8,24,384]{2,1,0:T(8,128)} %bitcast.9), calls=%async_computation | async-start | bytes 589824 | tf_op jit(solution)/shard_map/all_to_all | solution.py:53
  67.1 2.7 %collective-permute-start = (f32[2,24,128]{2,1,0:T(8,128)S(1)}, f32[2,24,128]{2,1,0:T(8,128)S(1)}, u32[]{:S(2)}, u32[]{:S(2)}) collective-permute-start(f32[2,24,128]{2,1,0:T(8,128)S(1)} %pad_maximum_fusion.4), channel_id=1, source_target_pairs={{0,1},{1,0},{2,3},{3,2},{4,5},{5,4},{6,7},{7,6},{8,9},{9,8},{10,11... | collective-permute-start | bytes 73736 | tf_op jit(solution)/shard_map/ppermute | solution.py:19
  77.8 2.8 %collective-permute-start.6 = (f32[2,24,128]{2,1,0:T(8,128)S(1)}, f32[2,24,128]{2,1,0:T(8,128)S(1)}, u32[]{:S(2)}, u32[]{:S(2)}) collective-permute-start(f32[2,24,128]{2,1,0:T(8,128)S(1)} %fusion.7), channel_id=1, source_target_pairs={{0,1},{1,0},{2,3},{3,2},{4,5},{5,4},{6,7},{7,6},{8,9},{9,8},{10,11... | collective-permute-start | bytes 73736 | tf_op jit(solution)/shard_map/ppermute | solution.py:19
  99.6 7.1 %collective-permute-start.7 = (f32[192,384]{1,0:T(8,128)S(1)}, f32[192,384]{1,0:T(8,128)S(1)}, u32[]{:S(2)}, u32[]{:S(2)}) collective-permute-start(f32[192,384]{1,0:T(8,128)S(1)} %all_gather.3), channel_id=1, source_target_pairs={{0,4},{4,0},{1,5},{5,1},{2,6},{6,2},{3,7},{7,3},{8,12},{12,8},{9,1... | collective-permute-start | bytes 884744 | tf_op jit(solution)/shard_map/ppermute | solution.py:14
  110.2 17.0 %collective-permute-start.8 = (f32[384,384]{0,1:T(8,128)S(1)}, f32[384,384]{0,1:T(8,128)}, u32[]{:S(2)}, u32[]{:S(2)}) collective-permute-start(f32[384,384]{0,1:T(8,128)S(1)} %dynamic_update_slice.19), channel_id=1, source_target_pairs={{0,8},{8,16},{16,24},{24,0},{1,9},{9,17},{17,25},{25,1},{2,10},{10... | collective-permute-start | bytes 1769480 | tf_op jit(solution)/shard_map/ppermute | solution.py:14
  110.3 18.1 %collective-permute-start.9 = (f32[384,384]{0,1:T(8,128)S(1)}, f32[384,384]{0,1:T(8,128)}, u32[]{:S(2)}, u32[]{:S(2)}) collective-permute-start(f32[384,384]{0,1:T(8,128)S(1)} %dynamic_update_slice.19), channel_id=1, source_target_pairs={{0,16},{8,24},{16,0},{24,8},{1,17},{9,25},{17,1},{25,9},{2,18},{10... | collective-permute-start | bytes 1769480 | tf_op jit(solution)/shard_map/ppermute | solution.py:14
  111.6 17.9 %collective-permute-start.10 = (f32[384,384]{0,1:T(8,128)S(1)}, f32[384,384]{0,1:T(8,128)}, u32[]{:S(2)}, u32[]{:S(2)}) collective-permute-start(f32[384,384]{0,1:T(8,128)S(1)} %dynamic_update_slice.19), channel_id=1, source_target_pairs={{0,24},{8,0},{16,8},{24,16},{1,25},{9,1},{17,9},{25,17},{2,26},{10... | collective-permute-start | bytes 1769480 | tf_op jit(solution)/shard_map/ppermute | solution.py:14
  114.8 28.9 %all-to-all-start.1 = ((f32[8,48,128]{2,1,0:T(8,128)}), f32[8,48,128]{2,1,0:T(8,128)S(1)}, u32[]{:S(2)}, u32[]{:S(2)}) async-start(f32[8,48,128]{2,1,0:T(8,128)} %bitcast.23), calls=%async_computation.1 | async-start | bytes 393216 | tf_op jit(solution)/shard_map/all_to_all | solution.py:53
  130.7 48.8 %collective-permute-start.11 = (f32[1536,384]{0,1:T(8,128)S(1)}, f32[1536,384]{0,1:T(8,128)}, u32[]{:S(2)}, u32[]{:S(2)}) collective-permute-start(f32[1536,384]{0,1:T(8,128)S(1)} %constant_dynamic-update-slice_fusion), channel_id=1, source_target_pairs={{0,2},{2,0},{1,3},{3,1},{4,6},{6,4},{5,7},{7,5},{8,10},{10,8},{9,1... | collective-permute-start | bytes 7077896 | tf_op jit(solution)/shard_map/ppermute | solution.py:19
  143.7 2.8 %collective-permute-start.12 = (f32[48,128]{1,0:T(8,128)S(1)}, f32[48,128]{1,0:T(8,128)S(1)}, u32[]{:S(2)}, u32[]{:S(2)}) collective-permute-start(f32[48,128]{1,0:T(8,128)S(1)} %reduce_sum.28), channel_id=1, source_target_pairs={{0,8},{8,0},{16,24},{24,16},{1,9},{9,1},{17,25},{25,17},{2,10},{10... | collective-permute-start | bytes 73736 | tf_op jit(solution)/shard_map/ppermute | solution.py:19
  146.5 4.2 %collective-permute-start.13 = (f32[48,128]{1,0:T(8,128)S(1)}, f32[48,128]{1,0:T(8,128)S(1)}, u32[]{:S(2)}, u32[]{:S(2)}) collective-permute-start(f32[48,128]{1,0:T(8,128)S(1)} %add.189), channel_id=1, source_target_pairs={{0,16},{8,24},{16,0},{24,8},{1,17},{9,25},{17,1},{25,9},{2,18},{10... | collective-permute-start | bytes 73736 | tf_op jit(solution)/shard_map/ppermute | solution.py:19
  150.7 4.2 %collective-permute-start.14 = (f32[48,128]{1,0:T(8,128)S(1)}, f32[48,128]{1,0:T(8,128)S(1)}, u32[]{:S(2)}, u32[]{:S(2)}) collective-permute-start(f32[48,128]{1,0:T(8,128)S(1)} %add.190), channel_id=1, source_target_pairs={{0,4},{4,0},{1,5},{5,1},{2,6},{6,2},{3,7},{7,3},{8,12},{12,8},{9,1... | collective-permute-start | bytes 73736 | tf_op jit(solution)/shard_map/ppermute | solution.py:19
  167.1 3.9 %collective-permute-start.15 = (f32[2,128,128]{2,1,0:T(8,128)S(1)}, f32[2,128,128]{2,1,0:T(8,128)S(1)}, u32[]{:S(2)}, u32[]{:S(2)}) collective-permute-start(f32[2,128,128]{2,1,0:T(8,128)S(1)} %fusion.26), channel_id=1, source_target_pairs={{0,1},{1,0},{2,3},{3,2},{4,5},{5,4},{6,7},{7,6},{8,9},{9,8},{10,11... | collective-permute-start | bytes 393224 | tf_op jit(solution)/shard_map/ppermute | solution.py:19
  171.5 7.1 %collective-permute-start.16 = (f32[2,192,128]{2,1,0:T(8,128)S(1)}, f32[2,192,128]{2,1,0:T(8,128)S(1)}, u32[]{:S(2)}, u32[]{:S(2)}) collective-permute-start(f32[2,192,128]{2,1,0:T(8,128)S(1)} %fusion.3), channel_id=1, source_target_pairs={{0,2},{2,0},{1,3},{3,1},{4,6},{6,4},{5,7},{7,5},{8,10},{10,8},{9,1... | collective-permute-start | bytes 589832 | tf_op jit(solution)/shard_map/ppermute | solution.py:19
  185.9 4.9 %copy-start.1 = (f32[2,3072,128]{2,1,0:T(8,128)S(1)}, f32[2,3072,128]{2,1,0:T(8,128)}, u32[]{:S(2)}) copy-start(f32[2,3072,128]{2,1,0:T(8,128)} %copy.25) | copy-start | bytes 9437188
